TPU v7x, 128 devices: a whole 4x4x4 slice. The times are simulated.
128 devices in a mesh: tm: 8 (over x, z_lo), dp: 16 (over z_hi, y, core).
Axes of the slice: x: 4, y: 4, z: 4 (z_hi: 2, z_lo: 2; z = z_hi * 2 + z_lo), core: 2. Of those that a mesh axis runs over, the one named last changes fastest.
Arguments:
- clips: bfloat16 [16, 32, 32, 64, 128], P('dp', 'tm'), may hold values from -6 to 6
- weight: bfloat16 [3, 3, 3, 128, 256], replicated, may hold values from -0.109375 to 0.109375
- bias: float32 [256], replicated, may hold values from -3 to 3
- out_grad: bfloat16 [16, 16, 16, 32, 256], P('dp', 'tm'), may hold values from -6 to 6
Outputs:
- features: bfloat16 [16, 16, 16, 32, 256], P('dp', 'tm')
- clips_grad: bfloat16 [16, 32, 32, 64, 128], P('dp', 'tm')
- weight_grad: float32 [3, 3, 3, 128, 256], replicated
- bias_grad: float32 [256], replicated
All inputs are finite; a program needn't handle non-finite values.
Results may differ from a plain program's by a relative error of at most 0.005.
Values may be sent and summed in bfloat16 or wider, within the bound.
No kernel may reach another device: no remote copies, remote signals or barrier semaphores. Data moves between devices by JAX's collectives and lax.ppermute only.
A program may use at most 64 MiB of HBM per device.

v0:
```python
import itertools
import math

import jax
import jax.numpy as jnp
from jax import lax
from jax.experimental import pallas as pl
from jax.experimental.pallas import tpu as pltpu
from jax.sharding import PartitionSpec as P


BF = jnp.bfloat16
F32 = jnp.float32
AXES = ("tm", "dp")
MIB = 1 << 20


def device_index(x, y, z, core):
    return (x * 2 + z % 2) * 16 + (z // 2) * 8 + y * 2 + core


PLACES = list(itertools.product(range(4), range(4), range(4), range(2)))
CORE_SWAP = [
    (device_index(x, y, z, c), device_index(x, y, z, 1 - c)) for x, y, z, c in PLACES
]
RING = (3, 2, 1, 0)
ROW_SWAP = [(device_index(x, y, z, c), device_index(x, RING[y], z, c)) for x, y, z, c in PLACES]
TEAMS = [
    [device_index(x, y, z, c) for x in (3, 2, 1, 0) for y in pair for z in (3, 2, 1, 0)]
    for pair in ((0, 1), (3, 2))
    for c in range(2)
]
TEAM = len(TEAMS[0])
SHARE = 3584 // TEAM


def dot(a, b, ca, cb):
    return lax.dot_general(a, b, (((ca,), (cb,)), ((), ())), preferred_element_type=F32)


def patches_of(x_ref, frame, stage, p_ref, slot):
    zeros = jnp.zeros((8, 128), F32)
    for s in range(4):
        stage[s, 0:8, :] = zeros
    p_ref[slot, 0:32, 0:384] = jnp.zeros((32, 384), BF)

    def step(k, carry):
        for s in range(4):
            stage[s, 8:72, :] = x_ref[0, frame, 4 * k + s].astype(F32)
        for s in range(4):
            taps = [stage[s, pl.ds(7 + j, 32, stride=2), :].astype(BF) for j in range(3)]
            half = 2 * k + s // 2
            here = pl.ds(pl.multiple_of(half * 32, 32), 32)
            below = pl.ds(pl.multiple_of(half * 32 + 32, 32), 32)
            for j in range(3):
                if s % 2 == 0:
                    p_ref[slot, here, 384 + 128 * j : 512 + 128 * j] = taps[j]
                else:
                    p_ref[slot, here, 768 + 128 * j : 896 + 128 * j] = taps[j]
                    p_ref[slot, below, 128 * j : 128 * j + 128] = taps[j]
        return carry

    lax.fori_loop(0, 8, step, 0)


def head_kernel(x_ref, w_ref, s_ref, x, w, stage, patches, sems):
    copies = [pltpu.make_async_copy(x_ref.at[0, frame], x.at[0, frame], sems.at[frame]) for frame in range(4)]
    copies += [pltpu.make_async_copy(w_ref.at[kt], w.at[kt], sems.at[4 + kt]) for kt in range(2)]
    for n in (2, 4, 3, 5, 0, 1):
        copies[n].start()
    for slot in range(2):
        copies[2 + slot].wait()
        patches_of(x, 2 + slot, stage, patches, slot)
    for slot in range(2):
        copies[4 + slot].wait()
    s_ref[...] = (
        dot(patches[0, 0:512], w[0], 1, 0) + dot(patches[1, 0:512], w[1], 1, 0)
    ).astype(BF)
    for n in range(2):
        copies[n].wait()


def gate(pre, grad):
    sig = jax.nn.sigmoid(pre)
    return pre * sig, grad * (sig * (1.0 + pre * (1.0 - sig)))


def body_kernel(
    x_ref, w_ref, b_ref, g_ref, feat_ref, pg_ref, pre_ref, out_ref, stage, patches, w, w_sems, *scratch
):
    loads = [pltpu.make_async_copy(w_ref.at[kt], w.at[kt], w_sems.at[kt]) for kt in range(3)]
    for load in loads:
        load.start()
    for slot in range(3):
        patches_of(x_ref, slot, stage, patches, slot)
    for load in loads:
        load.wait()
    bias = b_ref[...]
    pre_ref[...] = dot(patches[0, 0:512], w[2], 1, 0) + bias
    pre = bias
    for slot in range(3):
        pre = pre + dot(patches[slot, 0:512], w[slot], 1, 0)
    feat, grad = gate(pre, g_ref[0, 1].reshape(512, 256).astype(F32))
    feat_ref[...] = feat.astype(BF)
    pg_ref[...] = grad.astype(BF)
    back_body(w, (pg_ref,), 1, (((0, 1),),), out_ref, *scratch)


def first_kernel(pre_ref, s_ref, g_ref, feat_ref, pg_ref):
    feat, grad = gate(pre_ref[...] + s_ref[...].astype(F32), g_ref[0, 0].reshape(512, 256).astype(F32))
    feat_ref[...] = feat.astype(BF)
    pg_ref[...] = grad.astype(BF)


def put(core, out_ref, rows, value):
    value = value.astype(BF)
    out_ref[core, rows, :] = value[:, 0:128]
    out_ref[1 - core, rows, :] = value[:, 128:256]


def middle_kernel(
    core_ref,
    x_ref,
    w_ref,
    pg0_ref,
    pg1_ref,
    f0_ref,
    f1_ref,
    held_ref,
    feat_ref,
    q_ref,
    dw_ref,
    out_ref,
    grad_ref,
    stage,
    patches,
    w,
    own_sems,
    *scratch,
):
    copies = [
        pltpu.make_async_copy(ref, feat_ref.at[n], own_sems.at[n]) for n, ref in enumerate((f0_ref, f1_ref))
    ]
    loads = [pltpu.make_async_copy(w_ref.at[kt], w.at[kt], own_sems.at[2 + kt]) for kt in range(3)]
    for copy in loads + copies:
        copy.start()
    for slot in range(2):
        patches_of(x_ref, slot, stage, patches, slot)
        patches_of(x_ref, 2 + slot, stage, q_ref, slot)
    put(
        core_ref[0],
        out_ref,
        slice(0, 1152),
        dot(q_ref[0, 0:512], pg1_ref[...], 0, 0) + dot(patches[0, 0:512], pg0_ref[...], 0, 0),
    )
    total = jnp.sum(pg0_ref[...].astype(F32) + pg1_ref[...].astype(F32), axis=0, keepdims=True)
    put(core_ref[0], out_ref, slice(1152, 1280), jnp.broadcast_to(total, (128, 256)))
    dw_ref[0] = dot(patches[0, 0:512], pg1_ref[...], 0, 0)
    dw_ref[1] = dot(patches[1, 0:512], pg1_ref[...], 0, 0)
    for copy in loads:
        copy.wait()
    back_body(w, (pg0_ref, pg1_ref), 0, (((0, 2), (1, 0)),), grad_ref, *scratch)
    for copy in copies:
        copy.wait()


def weight_kernel(core_ref, q_ref, pn_ref, dw_ref, out_ref):
    for kt in range(2):
        put(
            core_ref[0],
            out_ref,
            slice(1152 * kt, 1152 * kt + 1152),
            dw_ref[kt] + dot(q_ref[kt, 0:512], pn_ref[...], 0, 0),
        )


def join_kernel(late_ref, late_got_ref, early_ref, early_got_ref, out_ref):
    for rows, kept, got in (
        (slice(0, 2304), late_ref, late_got_ref),
        (slice(2304, 3584), early_ref, early_got_ref),
    ):
        out_ref[rows, :] = (kept[0].astype(F32) + got[...].astype(F32)).astype(BF)


def put_half(half, src_ref, out_ref, wide, sems):
    copies = []
    for n in range(4):
        rows = slice(864 * n, 864 * n + 864)
        wide[rows, :] = src_ref[rows, :].astype(F32)
        there = out_ref.at[pl.ds(864 * n, 864), pl.ds(pl.multiple_of(half * 128, 128), 128)]
        copies.append(pltpu.make_async_copy(wide.at[rows, :], there, sems.at[n]))
        copies[n].start()
    return copies


def own_kernel(core_ref, own_ref, out_ref, wide, sems):
    for copy in put_half(core_ref[0], own_ref, out_ref, wide, sems):
        copy.wait()


def other_kernel(core_ref, own_ref, other_ref, held_ref, out_ref, bias_ref, wide, line, sems):
    own = own_ref[3456:3464, :].astype(F32)[0:1]
    other = other_ref[3456:3464, :].astype(F32)[0:1]
    first = core_ref[0] == 0
    line[:, 0:128] = jnp.where(first, own, other)
    line[:, 128:256] = jnp.where(first, other, own)
    bias_copy = pltpu.make_async_copy(line, bias_ref, sems.at[4])
    bias_copy.start()
    for copy in put_half(1 - core_ref[0], other_ref, out_ref, wide, sems):
        copy.wait()
    bias_copy.wait()


def back_body(w_ref, refs, first, sources, out_ref, pgs, even, odd, stage, held, sems):
    last = lax.broadcasted_iota(jnp.int32, (512, 256), 0) % 32 == 31
    for k, ref in enumerate(refs):
        here = ref[...]
        pgs[k, 0, 0:512] = here
        moved = jnp.where(last, 0.0, pltpu.roll(here.astype(F32), 511, 0))
        pgs[k, 1, 0:512] = moved.astype(BF)
        pgs[k, 0, 512:544] = jnp.zeros((32, 256), BF)
        pgs[k, 1, 512:544] = jnp.zeros((32, 256), BF)
    copies = []
    for frame, terms in enumerate(sources):
        for n, (k, kt) in enumerate(terms):
            def rows(kh, kw, count):
                start = 384 * kh + 128 * kw
                return w_ref[kt, start : start + 128 * count, :]

            e = dot(pgs[k, 0, 0:512], rows(1, 1, 2), 1, 1)
            o = dot(pgs[k, 0, 0:512], rows(2, 1, 2), 1, 1) + dot(pgs[k, 0, 32:544], rows(0, 1, 2), 1, 1)
            es = dot(pgs[k, 1, 0:512], rows(1, 0, 1), 1, 1)
            os = dot(pgs[k, 1, 0:512], rows(2, 0, 1), 1, 1) + dot(pgs[k, 1, 32:544], rows(0, 0, 1), 1, 1)
            if n == 0:
                even[...] = e
                odd[...] = o
            else:
                even[...] += e
                odd[...] += o
            even[:, 128:256] += es
            odd[:, 128:256] += os

        def step(h, carry):
            here = pl.ds(pl.multiple_of(h * 32, 32), 32)
            for s, acc in enumerate((even, odd)):
                stage[s, pl.ds(0, 32, stride=2), :] = acc[here, 0:128]
                stage[s, pl.ds(1, 32, stride=2), :] = acc[here, 128:256]
            for s in range(2):
                held[frame, 2 * h + s] = stage[s, 0:64, :].astype(BF)
            return carry

        lax.fori_loop(0, 16, step, 0)
        copies.append(pltpu.make_async_copy(held.at[frame], out_ref.at[0, first + frame], sems.at[frame]))
        copies[frame].start()
    for copy in copies:
        copy.wait()


def high_kernel(w_ref, pg1_ref, pn_ref, held_ref, out_ref, *scratch):
    back_body(w_ref, (pg1_ref, pn_ref), 2, (((0, 2), (1, 0)), ((1, 1),)), out_ref, *scratch)


JOINED = jax.ShapeDtypeStruct
VM = pl.BlockSpec(memory_space=pltpu.VMEM)
HB = pl.BlockSpec(memory_space=pltpu.HBM)
SM = pl.BlockSpec(memory_space=pltpu.SMEM)


def call(kernel, outs, scratch, limit, flops, specs, out_specs=None, aliases=None):
    moved = sum(math.prod(o.shape) * jnp.dtype(o.dtype).itemsize for o in outs)
    out_specs = out_specs or [VM] * len(outs)
    return pl.pallas_call(
        kernel,
        out_shape=outs if len(outs) > 1 else outs[0],
        in_specs=specs,
        out_specs=out_specs if len(outs) > 1 else out_specs[0],
        scratch_shapes=scratch,
        input_output_aliases=aliases or {},
        compiler_params=pltpu.CompilerParams(vmem_limit_bytes=limit * MIB),
        cost_estimate=pl.CostEstimate(flops=flops, bytes_accessed=2 * moved, transcendentals=0),
    )


def shape(*dims, dtype=BF):
    return jax.ShapeDtypeStruct(dims, dtype)


def in_hbm(value):
    return pltpu.with_memory_space_constraint(value, pltpu.HBM)


def passed_along(value, steps):
    count = lax.axis_size("tm")
    first, last = (max(0, -steps), min(count, count - steps))
    return lax.ppermute(value, "tm", [(source, source + steps) for source in range(first, last)])


def spread_over(value):
    return lax.all_to_all(
        value, AXES, split_axis=0, concat_axis=0, tiled=True, axis_index_groups=TEAMS
    )


def finish(core, own):
    other = lax.ppermute(own, AXES, CORE_SWAP)
    whole = shape(3456, 256, dtype=F32)
    wide = pltpu.VMEM((3456, 128), F32)
    held = call(own_kernel, [whole], [wide, pltpu.SemaphoreType.DMA((4,))], 8, 1 << 20, [SM, VM], [HB])(core, own)
    return call(
        other_kernel,
        [whole, shape(1, 256, dtype=F32)],
        [wide, pltpu.VMEM((1, 256), F32), pltpu.SemaphoreType.DMA((5,))],
        8,
        1 << 20,
        [SM, VM, VM, HB],
        [HB, HB],
        {3: 0},
    )(core, own, other, held)


def local(clips, weight, bias, out_grad):
    taps = weight.reshape(3, 1152, 256)
    unit = 2 * 512 * 1152 * 256
    stage = pltpu.VMEM((4, 72, 128), F32)
    part, x = call(
        head_kernel,
        [pltpu.VMEM((512, 256), BF), pltpu.VMEM((1, 4, 32, 64, 128), BF)],
        [pltpu.VMEM((2, 1152, 256), BF), stage, pltpu.VMEM((2, 544, 1152), BF), pltpu.SemaphoreType.DMA((6,))],
        16,
        2 * unit,
        [HB] * 2,
    )(in_hbm(clips), in_hbm(taps))
    prior = passed_along(part, 1)

    def grad_scratch(frames):
        return [
            pltpu.VMEM((2, 2, 544, 256), BF),
            pltpu.VMEM((512, 256), F32),
            pltpu.VMEM((512, 256), F32),
            pltpu.VMEM((2, 64, 128), F32),
            pltpu.VMEM((frames, 32, 64, 128), BF),
            pltpu.SemaphoreType.DMA((frames,)),
        ]

    grad_shape = shape(1, 4, 32, 64, 128)
    feat1, pg1, pre0, held = call(
        body_kernel,
        [
            pltpu.VMEM((512, 256), BF),
            pltpu.VMEM((512, 256), BF),
            pltpu.VMEM((512, 256), F32),
            grad_shape,
        ],
        [
            stage,
            pltpu.VMEM((3, 544, 1152), BF),
            pltpu.VMEM((3, 1152, 256), BF),
            pltpu.SemaphoreType.DMA((3,)),
        ]
        + grad_scratch(1),
        16,
        5 * unit,
        [VM, HB, VM, VM],
        [VM] * 3 + [HB],
    )(x, in_hbm(taps), bias.reshape(1, 256), out_grad)
    feat0, pg0 = call(
        first_kernel, [pltpu.VMEM((512, 256), BF), pltpu.VMEM((512, 256), BF)], [], 8, unit // 10, [VM] * 3
    )(pre0, prior, out_grad)
    after = passed_along(pg0, -1)
    core = (lax.axis_index("dp") % 2).astype(jnp.int32).reshape(1)
    features, q, dw, early, held = call(
        middle_kernel,
        [
            shape(2, 512, 256),
            pltpu.VMEM((2, 544, 1152), BF),
            pltpu.VMEM((2, 1152, 256), F32),
            pltpu.VMEM((2, 1280, 128), BF),
            grad_shape,
        ],
        [
            stage,
            pltpu.VMEM((2, 544, 1152), BF),
            pltpu.VMEM((3, 1152, 256), BF),
            pltpu.SemaphoreType.DMA((5,)),
        ]
        + grad_scratch(1),
        16,
        6 * unit,
        [SM, VM, HB] + [VM] * 4 + [HB],
        [HB, VM, VM, VM, HB],
        {7: 4},
    )(core, x, in_hbm(taps), pg0, pg1, feat0, feat1, held)
    early_got = lax.ppermute(early[1], AXES, CORE_SWAP)
    late = call(weight_kernel, [pltpu.VMEM((2, 2304, 128), BF)], [], 8, 2 * unit, [SM] + [VM] * 3)(core, q, after, dw)
    late_got = lax.ppermute(late[1], AXES, CORE_SWAP)
    mine = call(join_kernel, [JOINED((3584, 128), BF)], [], 8, unit // 10, [VM] * 4)(late, late_got, early, early_got)
    pieces = spread_over(mine.reshape(TEAM, SHARE, 128))
    clips_grad = call(
        high_kernel, [grad_shape], grad_scratch(2), 8, 4 * unit, [VM] * 3 + [HB], [HB], {3: 0}
    )(taps, pg1, after, held)
    positions = 1024 * lax.axis_size("tm") * lax.axis_size("dp")
    total = jnp.sum(pieces.astype(F32), axis=0)
    total = total + lax.ppermute(total, AXES, ROW_SWAP)
    total = (total * (1.0 / math.sqrt(positions))).astype(BF)
    own = spread_over(jnp.broadcast_to(total[None], (TEAM, SHARE, 128))).reshape(3584, 128)
    weight_grad, bias_grad = finish(core, own)
    features = features.reshape(1, 2, 16, 32, 256)
    return features, clips_grad, weight_grad.reshape(3, 3, 3, 128, 256), bias_grad.reshape(256)


def solution(mesh):
    in_specs = (P("dp", "tm", None, None, None), P(), P(), P("dp", "tm", None, None, None))
    out_specs = (P("dp", "tm", None, None, None), P("dp", "tm", None, None, None), P(), P())
    return jax.shard_map(local, mesh=mesh, in_specs=in_specs, out_specs=out_specs, check_vma=False)
```

profile of v0, /device:TPU:1, one launch (start us, length us, event | category | flops | bytes accessed | tf_op | source)
XLA Modules:
  0.0 79.0 jit_solution(9764657553464907768)
XLA Ops:
  0.6 0.0 copy-start.2
  0.6 0.0 copy-start.1
  0.7 2.6 %shard_map.75 = (bf16[512,256]{1,0:T(8,128)(2,1)S(1)}, bf16[1,4,32,64,128]{4,3,2,1,0:T(8,128)(2,1)S(1)}) custom-call(bf16[1,4,32,64,128]{4,3,2,1,0:T(8,128)(2,1)} %x_ref.1, bf16[3,1152,256]{2,1,0:T(8,128)(2,1)} %bitcast.12), custom_call_target="tpu_custom_call" | custom-call | flops 603979776 | bytes 4718592 | tf_op jit(solution)/shard_map/pallas_call | solution.py:325
  3.3 4.4 %collective-permute-start = (bf16[512,256]{1,0:T(8,128)(2,1)S(1)}, bf16[512,256]{1,0:T(8,128)(2,1)S(1)}, u32[]{:S(2)}, u32[]{:S(2)}) collective-permute-start(bf16[512,256]{1,0:T(8,128)(2,1)S(1)} %get-tuple-element.21), channel_id=1, source_target_pairs={{0,16},{16,32},{32,48},{48,64},{64,80},{80,96},{96,112},{1,17},{17... | collective-permute-start | bytes 786440 | tf_op jit(solution)/shard_map/ppermute | solution.py:295
  7.6 0.0 copy-done.2
  7.6 0.0 copy-done.1
  7.7 5.3 %shard_map.76 = (bf16[512,256]{1,0:T(8,128)(2,1)S(1)}, bf16[512,256]{1,0:T(8,128)(2,1)S(1)}, f32[512,256]{1,0:T(8,128)S(1)}, bf16[1,4,32,64,128]{4,3,2,1,0:T(8,128)(2,1)}) custom-call(bf16[1,4,32,64,128]{4,3,2,1,0:T(8,128)(2,1)S(1)} %get-tuple-element.19.x_ref, bf16[3,1152,256]{2,1,0:T(8,128)(2,1)} %bitcast.13, f32[1,256]{1,0:T(1,128)S(1)} %bitcast.20, ...), custom_call_target="tpu_custom_call" | custom-call | flops 1509949440 | bytes 6291456 | tf_op jit(solution)/shard_map/pallas_call | solution.py:346
  12.9 0.0 collective-permute-done.s_ref
  12.9 0.2 shard_map.77
  13.2 1.3 %collective-permute-start.1 = (bf16[512,256]{1,0:T(8,128)(2,1)S(1)}, bf16[512,256]{1,0:T(8,128)(2,1)S(1)}, u32[]{:S(2)}, u32[]{:S(2)}) collective-permute-start(bf16[512,256]{1,0:T(8,128)(2,1)S(1)} %get-tuple-element.22.pg0_ref), channel_id=1, source_target_pairs={{16,0},{32,16},{48,32},{64,48},{80,64},{96,80},{112,96},{17,1},{33... | collective-permute-start | bytes 786440 | tf_op jit(solution)/shard_map/ppermute | solution.py:295
  14.5 4.8 %shard_map.78 = (bf16[2,512,256]{2,1,0:T(8,128)(2,1)}, bf16[2,544,1152]{2,1,0:T(8,128)(2,1)S(1)}, f32[2,1152,256]{2,1,0:T(8,128)S(1)}, bf16[2,1280,128]{2,1,0:T(8,128)(2,1)S(1)}, bf16[1,4,32,64,128]{4,3,2,1,0:T(8,128)(2,1)}) custom-call(s32[1]{0:T(128)} %bitcast.core_ref, ...), custom_call_target="tpu_custom_call", output_to_operand_aliasing={{4}: (7, {})} | custom-call | flops 1811939328 | bytes 16285696 | tf_op jit(solution)/shard_map/pallas_call | solution.py:371
  19.4 2.7 %collective-permute-done.1.pn_ref = bf16[512,256]{1,0:T(8,128)(2,1)S(1)} collective-permute-done((bf16[512,256]{1,0:T(8,128)(2,1)S(1)}, bf16[512,256]{1,0:T(8,128)(2,1)S(1)}, u32[]{:S(2)}, u32[]{:S(2)}) %collective-permute-start.1) | collective-permute-done | bytes 262176 | tf_op jit(solution)/shard_map/ppermute | solution.py:295
  22.1 0.9 %shard_map.80.late_ref = bf16[2,2304,128]{2,1,0:T(8,128)(2,1)S(1)} custom-call(s32[1]{0:T(128)} %bitcast.core_ref, bf16[2,544,1152]{2,1,0:T(8,128)(2,1)S(1)} %get-tuple-element.29.q_ref, bf16[512,256]{1,0:T(8,128)(2,1)S(1)} %collective-permute-done.1.pn_ref, f32[2,1152,256]{2,1,0:T(8,128)S(1)} %get-tuple-element.30.dw_ref), custom_call_target="tpu_custom_call" | custom-call | flops 603979776 | bytes 2359296 | tf_op jit(solution)/shard_map/pallas_call | solution.py:394
  23.0 2.2 %collective-permute-start.2 = (bf16[2304,128]{1,0:T(8,128)(2,1)S(1)}, bf16[2304,128]{1,0:T(8,128)(2,1)S(1)}, u32[]{:S(2)}, u32[]{:S(2)}) collective-permute-start(bf16[2304,128]{1,0:T(8,128)(2,1)S(1)} %slice_bitcast_fusion), channel_id=1, source_target_pairs={{0,1},{1,0},{16,17},{17,16},{8,9},{9,8},{24,25},{25,24},{2,3},{3,2... | collective-permute-start | bytes 1769480 | tf_op jit(solution)/shard_map/ppermute | solution.py:395
  25.3 0.1 collective-permute-start.3
  25.4 2.0 %collective-permute-done.3.early_got_ref = bf16[1280,128]{1,0:T(8,128)(2,1)S(1)} collective-permute-done((bf16[1280,128]{1,0:T(8,128)(2,1)S(1)}, bf16[1280,128]{1,0:T(8,128)(2,1)S(1)}, u32[]{:S(2)}, u32[]{:S(2)}) %collective-permute-start.3) | collective-permute-done | bytes 327712 | tf_op jit(solution)/shard_map/ppermute | solution.py:393
  27.3 0.0 collective-permute-done.2.late_got_ref
  27.3 0.2 shard_map.81
  27.5 21.8 %all_to_all.10 = bf16[32,112,128]{2,1,0:T(8,128)(2,1)S(1)} all-to-all(bf16[32,112,128]{2,1,0:T(8,128)(2,1)S(1)} %bitcast.19), channel_id=1, replica_groups={{120,104,112,96,122,106,114,98,88,72,80,64,90,74,82,66,56,40,48,32,58,4..., dimensions={0} | all-to-all | bytes 1835008 | tf_op jit(solution)/shard_map/all_to_all | solution.py:299
  49.3 0.0 copy-start
  49.3 0.1 convert_reduce_fusion
  49.4 2.0 %collective-permute-start.4 = (f32[112,128]{1,0:T(8,128)S(1)}, f32[112,128]{1,0:T(8,128)S(1)}, u32[]{:S(2)}, u32[]{:S(2)}) collective-permute-start(f32[112,128]{1,0:T(8,128)S(1)} %convert_reduce_fusion), channel_id=1, source_target_pairs={{0,6},{1,7},{16,22},{17,23},{8,14},{9,15},{24,30},{25,31},{2,4},{3... | collective-permute-start | bytes 172040 | tf_op jit(solution)/shard_map/ppermute | solution.py:403
  51.4 2.3 %collective-permute-done.4 = f32[112,128]{1,0:T(8,128)S(1)} collective-permute-done((f32[112,128]{1,0:T(8,128)S(1)}, f32[112,128]{1,0:T(8,128)S(1)}, u32[]{:S(2)}, u32[]{:S(2)}) %collective-permute-start.4) | collective-permute-done | bytes 57376 | tf_op jit(solution)/shard_map/ppermute | solution.py:403
  53.8 0.1 broadcast_in_dim.2
  53.9 16.0 %all_to_all.11 = bf16[32,112,128]{2,1,0:T(8,128)(2,1)S(1)} all-to-all(bf16[32,112,128]{2,1,0:T(8,128)(2,1)S(1)} %broadcast_in_dim.2), channel_id=1, replica_groups={{120,104,112,96,122,106,114,98,88,72,80,64,90,74,82,66,56,40,48,32,58,4..., dimensions={0} | all-to-all | bytes 1835008 | tf_op jit(solution)/shard_map/all_to_all | solution.py:299
  69.9 3.7 %collective-permute-start.5 = (bf16[3584,128]{1,0:T(8,128)(2,1)S(1)}, bf16[3584,128]{1,0:T(8,128)(2,1)S(1)}, u32[]{:S(2)}, u32[]{:S(2)}) collective-permute-start(bf16[3584,128]{1,0:T(8,128)(2,1)S(1)} %bitcast.16), channel_id=1, source_target_pairs={{0,1},{1,0},{16,17},{17,16},{8,9},{9,8},{24,25},{25,24},{2,3},{3,2... | collective-permute-start | bytes 2752520 | tf_op jit(solution)/shard_map/ppermute | solution.py:305
  73.6 0.0 copy-done
  73.6 2.8 %shard_map.79 = bf16[1,4,32,64,128]{4,3,2,1,0:T(8,128)(2,1)} custom-call(bf16[3,1152,256]{2,1,0:T(8,128)(2,1)S(1)} %bitcast.15, bf16[512,256]{1,0:T(8,128)(2,1)S(1)} %get-tuple-element.23.pg1_ref, bf16[512,256]{1,0:T(8,128)(2,1)S(1)} %collective-permute-done.1.pn_ref, ...), custom_call_target="tpu_custom_call", output_to_operand_aliasing={{}: (3, {})} | custom-call | flops 1207959552 | bytes 4194304 | tf_op jit(solution)/shard_map/pallas_call | solution.py:398
  76.4 1.3 %shard_map.82.held_ref = f32[3456,256]{1,0:T(8,128)} custom-call(s32[1]{0:T(128)} %bitcast.core_ref, bf16[3584,128]{1,0:T(8,128)(2,1)S(1)} %bitcast.17), custom_call_target="tpu_custom_call" | custom-call | flops 1048576 | bytes 7077888 | tf_op jit(solution)/shard_map/pallas_call | solution.py:308
  77.7 0.0 collective-permute-done.5.other_ref
  77.7 1.3 %shard_map.83 = (f32[3456,256]{1,0:T(8,128)}, f32[1,256]{1,0:T(1,128)}) custom-call(s32[1]{0:T(128)} %bitcast.core_ref, bf16[3584,128]{1,0:T(8,128)(2,1)S(1)} %bitcast.18, bf16[3584,128]{1,0:T(8,128)(2,1)S(1)} %collective-permute-done.5.other_ref, f32[3456,256]{1,0:T(8,128)} %shard_map.82.held_ref), custom_call_target="tpu_custom_call", output_to_operand_aliasing={{0}: (3, {})} | custom-call | flops 1048576 | bytes 7079936 | tf_op jit(solution)/shard_map/pallas_call | solution.py:309
  (3 shorter events, 0.1 us)
Async XLA Ops:
  0.6 7.0 %copy-start.2 = (f32[256]{0:T(256)S(1)}, f32[256]{0:T(256)}, u32[]{:S(2)}) copy-start(f32[256]{0:T(256)} %param.6) | copy-start | bytes 3076
  0.6 7.0 %copy-start.1 = (bf16[1,2,16,32,256]{4,3,2,1,0:T(8,128)(2,1)S(1)}, bf16[1,2,16,32,256]{4,3,2,1,0:T(8,128)(2,1)}, u32[]{:S(2)}) copy-start(bf16[1,2,16,32,256]{4,3,2,1,0:T(8,128)(2,1)} %g_ref.3) | copy-start | bytes 1572868
  3.3 9.7 %collective-permute-start = (bf16[512,256]{1,0:T(8,128)(2,1)S(1)}, bf16[512,256]{1,0:T(8,128)(2,1)S(1)}, u32[]{:S(2)}, u32[]{:S(2)}) collective-permute-start(bf16[512,256]{1,0:T(8,128)(2,1)S(1)} %get-tuple-element.21), channel_id=1, source_target_pairs={{0,16},{16,32},{32,48},{48,64},{64,80},{80,96},{96,112},{1,17},{17... | collective-permute-start | bytes 786440 | tf_op jit(solution)/shard_map/ppermute | solution.py:295
  13.2 8.9 %collective-permute-start.1 = (bf16[512,256]{1,0:T(8,128)(2,1)S(1)}, bf16[512,256]{1,0:T(8,128)(2,1)S(1)}, u32[]{:S(2)}, u32[]{:S(2)}) collective-permute-start(bf16[512,256]{1,0:T(8,128)(2,1)S(1)} %get-tuple-element.22.pg0_ref), channel_id=1, source_target_pairs={{16,0},{32,16},{48,32},{64,48},{80,64},{96,80},{112,96},{17,1},{33... | collective-permute-start | bytes 786440 | tf_op jit(solution)/shard_map/ppermute | solution.py:295
  23.0 4.3 %collective-permute-start.2 = (bf16[2304,128]{1,0:T(8,128)(2,1)S(1)}, bf16[2304,128]{1,0:T(8,128)(2,1)S(1)}, u32[]{:S(2)}, u32[]{:S(2)}) collective-permute-start(bf16[2304,128]{1,0:T(8,128)(2,1)S(1)} %slice_bitcast_fusion), channel_id=1, source_target_pairs={{0,1},{1,0},{16,17},{17,16},{8,9},{9,8},{24,25},{25,24},{2,3},{3,2... | collective-permute-start | bytes 1769480 | tf_op jit(solution)/shard_map/ppermute | solution.py:395
  25.3 2.1 %collective-permute-start.3 = (bf16[1280,128]{1,0:T(8,128)(2,1)S(1)}, bf16[1280,128]{1,0:T(8,128)(2,1)S(1)}, u32[]{:S(2)}, u32[]{:S(2)}) collective-permute-start(bf16[1280,128]{1,0:T(8,128)(2,1)S(1)} %slice_bitcast_fusion.1), channel_id=1, source_target_pairs={{0,1},{1,0},{16,17},{17,16},{8,9},{9,8},{24,25},{25,24},{2,3},{3,2... | collective-permute-start | bytes 983048 | tf_op jit(solution)/shard_map/ppermute | solution.py:393
  49.3 24.3 %copy-start = (bf16[3,3,3,128,256]{4,3,2,1,0:T(8,128)(2,1)S(1)}, bf16[3,3,3,128,256]{4,3,2,1,0:T(8,128)(2,1)}, u32[]{:S(2)}) copy-start(bf16[3,3,3,128,256]{4,3,2,1,0:T(8,128)(2,1)} %param.5) | copy-start | bytes 5308420
  49.4 4.3 %collective-permute-start.4 = (f32[112,128]{1,0:T(8,128)S(1)}, f32[112,128]{1,0:T(8,128)S(1)}, u32[]{:S(2)}, u32[]{:S(2)}) collective-permute-start(f32[112,128]{1,0:T(8,128)S(1)} %convert_reduce_fusion), channel_id=1, source_target_pairs={{0,6},{1,7},{16,22},{17,23},{8,14},{9,15},{24,30},{25,31},{2,4},{3... | collective-permute-start | bytes 172040 | tf_op jit(solution)/shard_map/ppermute | solution.py:403
  69.9 7.8 %collective-permute-start.5 = (bf16[3584,128]{1,0:T(8,128)(2,1)S(1)}, bf16[3584,128]{1,0:T(8,128)(2,1)S(1)}, u32[]{:S(2)}, u32[]{:S(2)}) collective-permute-start(bf16[3584,128]{1,0:T(8,128)(2,1)S(1)} %bitcast.16), channel_id=1, source_target_pairs={{0,1},{1,0},{16,17},{17,16},{8,9},{9,8},{24,25},{25,24},{2,3},{3,2... | collective-permute-start | bytes 2752520 | tf_op jit(solution)/shard_map/ppermute | solution.py:305
where the time goes:
time: 79.2 us; the launch traced here: 79 us
  blocking collectives  37.7 us (48%)
  Pallas kernels  19.4 us (24%)
  starting transfers between devices  13.6 us (17%)
  waiting for transfers between devices  7.06 us (9%)
    all_to_all x2, blocking collectives, spread_over(): lax.all_to_all(value, AXES, split_axis=0, concat_axis=0, tiled=True, axis...  37.7 us
    ppermute x2, starting transfers between devices, passed_along(): lax.ppermute(value, 'tm', [(source, source + steps) for source in range(f...  5.67 us
    pallas_call x1, Pallas kernels, local(): call(body_kernel, [pltpu.VMEM((512, 256), BF), pltpu.VMEM((512, 256), BF)...  5.27 us
    pallas_call x1, Pallas kernels, local(): call(middle_kernel, [shape(2, 512, 256), pltpu.VMEM((2, 544, 1152), BF),...  4.84 us
    ppermute x1, starting transfers between devices, finish(): other = lax.ppermute(own, AXES, CORE_SWAP)  3.68 us
    pallas_call x1, Pallas kernels, local(): call(high_kernel, [grad_shape], grad_scratch(2), 8, 4 * unit, [VM] * 3 +...  2.82 us
    ppermute x2, waiting for transfers between devices, passed_along(): lax.ppermute(value, 'tm', [(source, source + steps) for source in range(f...  2.74 us
    pallas_call x1, Pallas kernels, local(): call(head_kernel, [pltpu.VMEM((512, 256), BF), pltpu.VMEM((1, 4, 32, 64,...  2.6 us
  transfers between devices with their start and end apart: 6, of which 3 were waited for; matrix products, arithmetic and copies ran while one was open for 0% of the time, Pallas kernels for 18%

commit v1 on v0

--- a/solution.py
+++ b/solution.py
@@ -66,11 +66,13 @@
 def head_kernel(x_ref, w_ref, s_ref, x, w, stage, patches, sems):
     copies = [pltpu.make_async_copy(x_ref.at[0, frame], x.at[0, frame], sems.at[frame]) for frame in range(4)]
     copies += [pltpu.make_async_copy(w_ref.at[kt], w.at[kt], sems.at[4 + kt]) for kt in range(2)]
-    for n in (2, 4, 3, 5, 0, 1):
+    for n in (2, 3, 4, 5):
         copies[n].start()
     for slot in range(2):
         copies[2 + slot].wait()
         patches_of(x, 2 + slot, stage, patches, slot)
+    for n in range(2):
+        copies[n].start()
     for slot in range(2):
         copies[4 + slot].wait()
     s_ref[...] = (
@@ -141,7 +143,7 @@
     copies = [
         pltpu.make_async_copy(ref, feat_ref.at[n], own_sems.at[n]) for n, ref in enumerate((f0_ref, f1_ref))
     ]
-    loads = [pltpu.make_async_copy(w_ref.at[kt], w.at[kt], own_sems.at[2 + kt]) for kt in range(3)]
+    loads = [pltpu.make_async_copy(w_ref.at[kt], w.at[kt], own_sems.at[2 + kt]) for kt in (2, 0)]
     for copy in loads + copies:
         copy.start()
     for slot in range(2):

time: 79.2 us -> 79.5 us (level)
  no operation moved by 1% of the time
where the time goes in v1:
time: 79.5 us; the launch traced here: 79.2 us
  blocking collectives  37.7 us (47%)
  Pallas kernels  19.7 us (25%)
  starting transfers between devices  13.6 us (17%)
  waiting for transfers between devices  7.06 us (9%)
    all_to_all x2, blocking collectives, spread_over(): lax.all_to_all(value, AXES, split_axis=0, concat_axis=0, tiled=True, axis...  37.7 us
    ppermute x2, starting transfers between devices, passed_along(): lax.ppermute(value, 'tm', [(source, source + steps) for source in range(f...  5.67 us
    pallas_call x1, Pallas kernels, local(): call(body_kernel, [pltpu.VMEM((512, 256), BF), pltpu.VMEM((512, 256), BF)...  5.27 us
    pallas_call x1, Pallas kernels, local(): call(middle_kernel, [shape(2, 512, 256), pltpu.VMEM((2, 544, 1152), BF),...  4.84 us
    ppermute x1, starting transfers between devices, finish(): other = lax.ppermute(own, AXES, CORE_SWAP)  3.68 us
    pallas_call x1, Pallas kernels, local(): call(head_kernel, [pltpu.VMEM((512, 256), BF), pltpu.VMEM((1, 4, 32, 64,...  2.86 us
    pallas_call x1, Pallas kernels, local(): call(high_kernel, [grad_shape], grad_scratch(2), 8, 4 * unit, [VM] * 3 +...  2.81 us
    ppermute x2, waiting for transfers between devices, passed_along(): lax.ppermute(value, 'tm', [(source, source + steps) for source in range(f...  2.74 us
  transfers between devices with their start and end apart: 6, of which 3 were waited for; matrix products, arithmetic and copies ran while one was open for 0% of the time, Pallas kernels for 18%

profile of v1, /device:TPU:1, one launch (start us, length us, event | category | flops | bytes accessed | tf_op | source)
XLA Modules:
  0.0 79.2 jit_solution(6331955708052767875)
XLA Ops:
  0.6 0.0 copy-start.2
  0.6 0.0 copy-start.1
  0.7 2.9 %shard_map.75 = (bf16[512,256]{1,0:T(8,128)(2,1)S(1)}, bf16[1,4,32,64,128]{4,3,2,1,0:T(8,128)(2,1)S(1)}) custom-call(bf16[1,4,32,64,128]{4,3,2,1,0:T(8,128)(2,1)} %x_ref.1, bf16[3,1152,256]{2,1,0:T(8,128)(2,1)} %bitcast.12), custom_call_target="tpu_custom_call" | custom-call | flops 603979776 | bytes 4718592 | tf_op jit(solution)/shard_map/pallas_call | solution.py:327
  3.5 4.4 %collective-permute-start = (bf16[512,256]{1,0:T(8,128)(2,1)S(1)}, bf16[512,256]{1,0:T(8,128)(2,1)S(1)}, u32[]{:S(2)}, u32[]{:S(2)}) collective-permute-start(bf16[512,256]{1,0:T(8,128)(2,1)S(1)} %get-tuple-element.21), channel_id=1, source_target_pairs={{0,16},{16,32},{32,48},{48,64},{64,80},{80,96},{96,112},{1,17},{17... | collective-permute-start | bytes 786440 | tf_op jit(solution)/shard_map/ppermute | solution.py:297
  7.9 0.0 copy-done.2
  7.9 0.0 copy-done.1
  7.9 5.3 %shard_map.76 = (bf16[512,256]{1,0:T(8,128)(2,1)S(1)}, bf16[512,256]{1,0:T(8,128)(2,1)S(1)}, f32[512,256]{1,0:T(8,128)S(1)}, bf16[1,4,32,64,128]{4,3,2,1,0:T(8,128)(2,1)}) custom-call(bf16[1,4,32,64,128]{4,3,2,1,0:T(8,128)(2,1)S(1)} %get-tuple-element.19.x_ref, bf16[3,1152,256]{2,1,0:T(8,128)(2,1)} %bitcast.13, f32[1,256]{1,0:T(1,128)S(1)} %bitcast.20, ...), custom_call_target="tpu_custom_call" | custom-call | flops 1509949440 | bytes 6291456 | tf_op jit(solution)/shard_map/pallas_call | solution.py:348
  13.2 0.0 collective-permute-done.s_ref
  13.2 0.2 shard_map.77
  13.5 1.3 %collective-permute-start.1 = (bf16[512,256]{1,0:T(8,128)(2,1)S(1)}, bf16[512,256]{1,0:T(8,128)(2,1)S(1)}, u32[]{:S(2)}, u32[]{:S(2)}) collective-permute-start(bf16[512,256]{1,0:T(8,128)(2,1)S(1)} %get-tuple-element.22.pg0_ref), channel_id=1, source_target_pairs={{16,0},{32,16},{48,32},{64,48},{80,64},{96,80},{112,96},{17,1},{33... | collective-permute-start | bytes 786440 | tf_op jit(solution)/shard_map/ppermute | solution.py:297
  14.8 4.8 %shard_map.78 = (bf16[2,512,256]{2,1,0:T(8,128)(2,1)}, bf16[2,544,1152]{2,1,0:T(8,128)(2,1)S(1)}, f32[2,1152,256]{2,1,0:T(8,128)S(1)}, bf16[2,1280,128]{2,1,0:T(8,128)(2,1)S(1)}, bf16[1,4,32,64,128]{4,3,2,1,0:T(8,128)(2,1)}) custom-call(s32[1]{0:T(128)} %bitcast.core_ref, ...), custom_call_target="tpu_custom_call", output_to_operand_aliasing={{4}: (7, {})} | custom-call | flops 1811939328 | bytes 16285696 | tf_op jit(solution)/shard_map/pallas_call | solution.py:373
  19.6 2.7 %collective-permute-done.1.pn_ref = bf16[512,256]{1,0:T(8,128)(2,1)S(1)} collective-permute-done((bf16[512,256]{1,0:T(8,128)(2,1)S(1)}, bf16[512,256]{1,0:T(8,128)(2,1)S(1)}, u32[]{:S(2)}, u32[]{:S(2)}) %collective-permute-start.1) | collective-permute-done | bytes 262176 | tf_op jit(solution)/shard_map/ppermute | solution.py:297
  22.4 0.9 %shard_map.80.late_ref = bf16[2,2304,128]{2,1,0:T(8,128)(2,1)S(1)} custom-call(s32[1]{0:T(128)} %bitcast.core_ref, bf16[2,544,1152]{2,1,0:T(8,128)(2,1)S(1)} %get-tuple-element.29.q_ref, bf16[512,256]{1,0:T(8,128)(2,1)S(1)} %collective-permute-done.1.pn_ref, f32[2,1152,256]{2,1,0:T(8,128)S(1)} %get-tuple-element.30.dw_ref), custom_call_target="tpu_custom_call" | custom-call | flops 603979776 | bytes 2359296 | tf_op jit(solution)/shard_map/pallas_call | solution.py:396
  23.3 2.2 %collective-permute-start.2 = (bf16[2304,128]{1,0:T(8,128)(2,1)S(1)}, bf16[2304,128]{1,0:T(8,128)(2,1)S(1)}, u32[]{:S(2)}, u32[]{:S(2)}) collective-permute-start(bf16[2304,128]{1,0:T(8,128)(2,1)S(1)} %slice_bitcast_fusion), channel_id=1, source_target_pairs={{0,1},{1,0},{16,17},{17,16},{8,9},{9,8},{24,25},{25,24},{2,3},{3,2... | collective-permute-start | bytes 1769480 | tf_op jit(solution)/shard_map/ppermute | solution.py:397
  25.5 0.1 collective-permute-start.3
  25.6 2.0 %collective-permute-done.3.early_got_ref = bf16[1280,128]{1,0:T(8,128)(2,1)S(1)} collective-permute-done((bf16[1280,128]{1,0:T(8,128)(2,1)S(1)}, bf16[1280,128]{1,0:T(8,128)(2,1)S(1)}, u32[]{:S(2)}, u32[]{:S(2)}) %collective-permute-start.3) | collective-permute-done | bytes 327712 | tf_op jit(solution)/shard_map/ppermute | solution.py:395
  27.6 0.0 collective-permute-done.2.late_got_ref
  27.6 0.2 shard_map.81
  27.8 21.8 %all_to_all.10 = bf16[32,112,128]{2,1,0:T(8,128)(2,1)S(1)} all-to-all(bf16[32,112,128]{2,1,0:T(8,128)(2,1)S(1)} %bitcast.19), channel_id=1, replica_groups={{120,104,112,96,122,106,114,98,88,72,80,64,90,74,82,66,56,40,48,32,58,4..., dimensions={0} | all-to-all | bytes 1835008 | tf_op jit(solution)/shard_map/all_to_all | solution.py:301
  49.6 0.0 copy-start
  49.6 0.1 convert_reduce_fusion
  49.7 2.0 %collective-permute-start.4 = (f32[112,128]{1,0:T(8,128)S(1)}, f32[112,128]{1,0:T(8,128)S(1)}, u32[]{:S(2)}, u32[]{:S(2)}) collective-permute-start(f32[112,128]{1,0:T(8,128)S(1)} %convert_reduce_fusion), channel_id=1, source_target_pairs={{0,6},{1,7},{16,22},{17,23},{8,14},{9,15},{24,30},{25,31},{2,4},{3... | collective-permute-start | bytes 172040 | tf_op jit(solution)/shard_map/ppermute | solution.py:405
  51.7 2.3 %collective-permute-done.4 = f32[112,128]{1,0:T(8,128)S(1)} collective-permute-done((f32[112,128]{1,0:T(8,128)S(1)}, f32[112,128]{1,0:T(8,128)S(1)}, u32[]{:S(2)}, u32[]{:S(2)}) %collective-permute-start.4) | collective-permute-done | bytes 57376 | tf_op jit(solution)/shard_map/ppermute | solution.py:405
  54.0 0.1 broadcast_in_dim.2
  54.2 16.0 %all_to_all.11 = bf16[32,112,128]{2,1,0:T(8,128)(2,1)S(1)} all-to-all(bf16[32,112,128]{2,1,0:T(8,128)(2,1)S(1)} %broadcast_in_dim.2), channel_id=1, replica_groups={{120,104,112,96,122,106,114,98,88,72,80,64,90,74,82,66,56,40,48,32,58,4..., dimensions={0} | all-to-all | bytes 1835008 | tf_op jit(solution)/shard_map/all_to_all | solution.py:301
  70.1 3.7 %collective-permute-start.5 = (bf16[3584,128]{1,0:T(8,128)(2,1)S(1)}, bf16[3584,128]{1,0:T(8,128)(2,1)S(1)}, u32[]{:S(2)}, u32[]{:S(2)}) collective-permute-start(bf16[3584,128]{1,0:T(8,128)(2,1)S(1)} %bitcast.16), channel_id=1, source_target_pairs={{0,1},{1,0},{16,17},{17,16},{8,9},{9,8},{24,25},{25,24},{2,3},{3,2... | collective-permute-start | bytes 2752520 | tf_op jit(solution)/shard_map/ppermute | solution.py:307
  73.8 0.0 copy-done
  73.8 2.8 %shard_map.79 = bf16[1,4,32,64,128]{4,3,2,1,0:T(8,128)(2,1)} custom-call(bf16[3,1152,256]{2,1,0:T(8,128)(2,1)S(1)} %bitcast.15, bf16[512,256]{1,0:T(8,128)(2,1)S(1)} %get-tuple-element.23.pg1_ref, bf16[512,256]{1,0:T(8,128)(2,1)S(1)} %collective-permute-done.1.pn_ref, ...), custom_call_target="tpu_custom_call", output_to_operand_aliasing={{}: (3, {})} | custom-call | flops 1207959552 | bytes 4194304 | tf_op jit(solution)/shard_map/pallas_call | solution.py:400
  76.7 1.3 %shard_map.82.held_ref = f32[3456,256]{1,0:T(8,128)} custom-call(s32[1]{0:T(128)} %bitcast.core_ref, bf16[3584,128]{1,0:T(8,128)(2,1)S(1)} %bitcast.17), custom_call_target="tpu_custom_call" | custom-call | flops 1048576 | bytes 7077888 | tf_op jit(solution)/shard_map/pallas_call | solution.py:310
  77.9 0.0 collective-permute-done.5.other_ref
  77.9 1.3 %shard_map.83 = (f32[3456,256]{1,0:T(8,128)}, f32[1,256]{1,0:T(1,128)}) custom-call(s32[1]{0:T(128)} %bitcast.core_ref, bf16[3584,128]{1,0:T(8,128)(2,1)S(1)} %bitcast.18, bf16[3584,128]{1,0:T(8,128)(2,1)S(1)} %collective-permute-done.5.other_ref, f32[3456,256]{1,0:T(8,128)} %shard_map.82.held_ref), custom_call_target="tpu_custom_call", output_to_operand_aliasing={{0}: (3, {})} | custom-call | flops 1048576 | bytes 7079936 | tf_op jit(solution)/shard_map/pallas_call | solution.py:311
  (3 shorter events, 0.1 us)
Async XLA Ops:
  0.6 7.3 %copy-start.2 = (f32[256]{0:T(256)S(1)}, f32[256]{0:T(256)}, u32[]{:S(2)}) copy-start(f32[256]{0:T(256)} %param.6) | copy-start | bytes 3076
  0.6 7.3 %copy-start.1 = (bf16[1,2,16,32,256]{4,3,2,1,0:T(8,128)(2,1)S(1)}, bf16[1,2,16,32,256]{4,3,2,1,0:T(8,128)(2,1)}, u32[]{:S(2)}) copy-start(bf16[1,2,16,32,256]{4,3,2,1,0:T(8,128)(2,1)} %g_ref.3) | copy-start | bytes 1572868
  3.5 9.7 %collective-permute-start = (bf16[512,256]{1,0:T(8,128)(2,1)S(1)}, bf16[512,256]{1,0:T(8,128)(2,1)S(1)}, u32[]{:S(2)}, u32[]{:S(2)}) collective-permute-start(bf16[512,256]{1,0:T(8,128)(2,1)S(1)} %get-tuple-element.21), channel_id=1, source_target_pairs={{0,16},{16,32},{32,48},{48,64},{64,80},{80,96},{96,112},{1,17},{17... | collective-permute-start | bytes 786440 | tf_op jit(solution)/shard_map/ppermute | solution.py:297
  13.5 8.9 %collective-permute-start.1 = (bf16[512,256]{1,0:T(8,128)(2,1)S(1)}, bf16[512,256]{1,0:T(8,128)(2,1)S(1)}, u32[]{:S(2)}, u32[]{:S(2)}) collective-permute-start(bf16[512,256]{1,0:T(8,128)(2,1)S(1)} %get-tuple-element.22.pg0_ref), channel_id=1, source_target_pairs={{16,0},{32,16},{48,32},{64,48},{80,64},{96,80},{112,96},{17,1},{33... | collective-permute-start | bytes 786440 | tf_op jit(solution)/shard_map/ppermute | solution.py:297
  23.3 4.3 %collective-permute-start.2 = (bf16[2304,128]{1,0:T(8,128)(2,1)S(1)}, bf16[2304,128]{1,0:T(8,128)(2,1)S(1)}, u32[]{:S(2)}, u32[]{:S(2)}) collective-permute-start(bf16[2304,128]{1,0:T(8,128)(2,1)S(1)} %slice_bitcast_fusion), channel_id=1, source_target_pairs={{0,1},{1,0},{16,17},{17,16},{8,9},{9,8},{24,25},{25,24},{2,3},{3,2... | collective-permute-start | bytes 1769480 | tf_op jit(solution)/shard_map/ppermute | solution.py:397
  25.5 2.1 %collective-permute-start.3 = (bf16[1280,128]{1,0:T(8,128)(2,1)S(1)}, bf16[1280,128]{1,0:T(8,128)(2,1)S(1)}, u32[]{:S(2)}, u32[]{:S(2)}) collective-permute-start(bf16[1280,128]{1,0:T(8,128)(2,1)S(1)} %slice_bitcast_fusion.1), channel_id=1, source_target_pairs={{0,1},{1,0},{16,17},{17,16},{8,9},{9,8},{24,25},{25,24},{2,3},{3,2... | collective-permute-start | bytes 983048 | tf_op jit(solution)/shard_map/ppermute | solution.py:395
  49.6 24.3 %copy-start = (bf16[3,3,3,128,256]{4,3,2,1,0:T(8,128)(2,1)S(1)}, bf16[3,3,3,128,256]{4,3,2,1,0:T(8,128)(2,1)}, u32[]{:S(2)}) copy-start(bf16[3,3,3,128,256]{4,3,2,1,0:T(8,128)(2,1)} %param.5) | copy-start | bytes 5308420
  49.7 4.3 %collective-permute-start.4 = (f32[112,128]{1,0:T(8,128)S(1)}, f32[112,128]{1,0:T(8,128)S(1)}, u32[]{:S(2)}, u32[]{:S(2)}) collective-permute-start(f32[112,128]{1,0:T(8,128)S(1)} %convert_reduce_fusion), channel_id=1, source_target_pairs={{0,6},{1,7},{16,22},{17,23},{8,14},{9,15},{24,30},{25,31},{2,4},{3... | collective-permute-start | bytes 172040 | tf_op jit(solution)/shard_map/ppermute | solution.py:405
  70.1 7.8 %collective-permute-start.5 = (bf16[3584,128]{1,0:T(8,128)(2,1)S(1)}, bf16[3584,128]{1,0:T(8,128)(2,1)S(1)}, u32[]{:S(2)}, u32[]{:S(2)}) collective-permute-start(bf16[3584,128]{1,0:T(8,128)(2,1)S(1)} %bitcast.16), channel_id=1, source_target_pairs={{0,1},{1,0},{16,17},{17,16},{8,9},{9,8},{24,25},{25,24},{2,3},{3,2... | collective-permute-start | bytes 2752520 | tf_op jit(solution)/shard_map/ppermute | solution.py:307
